TPU v7x, 32 devices: a whole 2x2x4 slice. The times are simulated.
32 devices in a mesh: group: 2 (over x), seq: 16 (over z, y, core).
Axes of the slice: x: 2, y: 2, z: 4, core: 2. Of those that a mesh axis runs over, the one named last changes fastest.
Arguments:
- queries: bfloat16 [8192, 768], P(('group', 'seq')), parts along dimension 0, may hold values from -6 to 6
- key_rows: bfloat16 [8192, 768], P(('group', 'seq')), parts along dimension 0, may hold values from -6 to 6
- value_rows: bfloat16 [8192, 768], P(('group', 'seq')), parts along dimension 0, may hold values from -20 to 20
- dilation: int32 [12], replicated, may hold values from 2 to 30, as said below
- global_rows: int32 [128], P('group'), parts along dimension 0, may hold values from 0 to 4095, as said below
- out_weight: bfloat16 [768, 1536], replicated, may hold values from -0.21875 to 0.21875
- mlp_up: bfloat16 [1536, 3072], P('seq'), may hold values from -0.15625 to 0.15625
- mlp_down: bfloat16 [3072, 1536], P('seq'), may hold values from -0.109375 to 0.109375
Outputs:
- attended: bfloat16 [8192, 1536], P(('group', 'seq')), parts along dimension 0
- mlp_out: bfloat16 [8192, 1536], P(('group', 'seq')), parts along dimension 0
There are 2 independent parts, one for each index of `group`. A program takes and returns all parts, laid end to end along the dimension named above; an argument that names none is the same for every part. Nothing has to cross between parts.
Inputs may be any that keep to these rules, and one draw needn't show every extreme that they name: `dilation`: each offset is a multiple of 2; some head has the smallest and some the largest. `global_rows`: distinct positions.
All inputs are finite; a program needn't handle non-finite values.
Results may differ from a plain program's by a relative error of at most 0.0071.
Values may be sent and summed in bfloat16 or wider, within the bound.
A program may use at most 192 MiB of HBM per device.

v0:
```python
import jax
import jax.numpy as jnp
from jax import lax
from jax.sharding import PartitionSpec as P

H = 12
DH = 64
BLK = 128
GLOBALS = 64


def with_halo(cells, sides, width):
    for axis, dim in sides:
        count = lax.axis_size(axis)
        head = lax.slice_in_dim(cells, 0, width, axis=dim)
        tail = lax.slice_in_dim(cells, cells.shape[dim] - width, cells.shape[dim], axis=dim)
        cells = jnp.concatenate(
            [
                lax.ppermute(tail, axis, [(i, (i + 1) % count) for i in range(count)]),
                cells,
                lax.ppermute(head, axis, [((i + 1) % count, i) for i in range(count)]),
            ],
            axis=dim,
        )
    return cells


def passed_along(value, axis, steps):
    count = lax.axis_size(axis)
    pairs = [(source, (source + steps) % count) for source in range(count)]
    return lax.ppermute(value, axis, pairs)


def merged_2(part, axis, combine):
    gathered = jax.tree.map(lambda a: lax.all_gather(a, axis), part)

    def take(source):
        return jax.tree.map(lambda a: lax.dynamic_index_in_dim(a, source, 0, False), gathered)

    return lax.fori_loop(
        1, lax.axis_size(axis), lambda source, state: combine(state, take(source)), take(0)
    )


def attend_blocks(query_blocks, local_keys, local_values, glob_keys, glob_values):
    count = query_blocks.shape[0]
    keys_all = jnp.concatenate(
        [local_keys, jnp.broadcast_to(glob_keys[None], (count,) + glob_keys.shape)], axis=1
    )
    values_all = jnp.concatenate(
        [local_values, jnp.broadcast_to(glob_values[None], (count,) + glob_values.shape)], axis=1
    )
    scores = jnp.einsum(
        "nqhd,nkhd->nhqk", query_blocks, keys_all, preferred_element_type=jnp.float32
    ) * DH ** (-0.5)
    peak = jnp.max(scores, axis=-1, keepdims=True)
    exp_terms = jnp.exp(scores - peak)
    totals = jnp.sum(exp_terms, axis=-1, keepdims=True)
    weights = (exp_terms / totals).astype(jnp.bfloat16)
    return jnp.einsum("nhqk,nkhd->nqhd", weights, values_all, preferred_element_type=jnp.float32)


def select_heads(chosen, arrived, current):
    shaped = current.shape
    head_mask = chosen[None, None, :, None]
    merged = jnp.where(
        head_mask,
        arrived.reshape(shaped[0], shaped[1], H, DH),
        current.reshape(shaped[0], shaped[1], H, DH),
    )
    return merged.reshape(shaped)


def join_partials(first, second):
    peak_first, total_first, numer_first = first
    peak_second, total_second, numer_second = second
    highest = jnp.maximum(peak_first, peak_second)
    scale_first = jnp.exp(peak_first - highest)
    scale_second = jnp.exp(peak_second - highest)
    return (
        highest,
        total_first * scale_first + total_second * scale_second,
        numer_first * scale_first[:, :, None] + numer_second * scale_second[:, :, None],
    )


def per_device(queries, key_rows, value_rows, dilation, global_rows, out_weight, mlp_up, mlp_down):
    tok_rows = queries.shape[0]
    blocks = tok_rows // BLK
    devices = lax.axis_size("seq")
    stacked = jnp.stack([key_rows, value_rows])
    padded = with_halo(stacked, (("seq", 1),), BLK)
    dev_hops = dilation // blocks
    current = stacked
    for bit_level in range((devices - 1).bit_length()):
        arrived = passed_along(current, "seq", -(1 << bit_level))
        chosen = dev_hops >> bit_level & 1 == 1
        current = select_heads(chosen, arrived, current)
    start = lax.axis_index("seq") * tok_rows
    offsets = global_rows - start
    onehot = offsets[:, None] == jnp.arange(tok_rows, dtype=jnp.int32)[None, :]
    picker = onehot.astype(jnp.bfloat16)
    picked = (
        jnp.dot(picker, queries, preferred_element_type=jnp.float32),
        jnp.dot(picker, key_rows, preferred_element_type=jnp.float32),
        jnp.dot(picker, value_rows, preferred_element_type=jnp.float32),
    )
    glob_q, glob_k, glob_v = lax.psum((picked[0], picked[1], picked[2]), "seq")
    glob_query = glob_q.astype(jnp.bfloat16).reshape(GLOBALS, H, DH)
    glob_keys = glob_k.astype(jnp.bfloat16).reshape(GLOBALS, H, DH)
    glob_values = glob_v.astype(jnp.bfloat16).reshape(GLOBALS, H, DH)
    grid = padded.reshape(2, blocks + 2, BLK, H, DH)
    dilated = current.reshape(2, blocks, BLK, H, DH)
    local_set = jnp.concatenate([grid[:, :-2], grid[:, 1:-1], grid[:, 2:], dilated], axis=2)
    attended_local = attend_blocks(
        queries.reshape(blocks, BLK, H, DH), local_set[0], local_set[1], glob_keys, glob_values
    ).reshape(tok_rows, H * DH)
    scores = jnp.einsum(
        "ghd,thd->hgt",
        glob_query,
        key_rows.reshape(tok_rows, H, DH),
        preferred_element_type=jnp.float32,
    ) * DH ** (-0.5)
    peak = jnp.max(scores, axis=2)
    exp_terms = jnp.exp(scores - peak[:, :, None])
    totals = jnp.sum(exp_terms, axis=2)
    numerators = jnp.einsum(
        "hgt,thd->hgd",
        exp_terms,
        value_rows.astype(jnp.float32).reshape(tok_rows, H, DH),
        precision=lax.Precision.HIGHEST,
    )
    peak, totals, numerators = merged_2((peak, totals, numerators), "seq", join_partials)
    glob_out = (numerators / totals[:, :, None]).transpose(1, 0, 2).reshape(GLOBALS, H * DH)
    onehot_float = onehot.astype(jnp.float32)
    placed = jnp.dot(onehot_float.T, glob_out, precision=lax.Precision.HIGHEST)
    owned_rows = jnp.sum(onehot_float, axis=0) > 0.5
    attention = jnp.where(owned_rows[:, None], placed, attended_local).astype(jnp.bfloat16)
    attended = jnp.dot(attention, out_weight, preferred_element_type=jnp.float32).astype(
        jnp.bfloat16
    )
    columns = attended
    pre_act = jnp.dot(
        columns,
        lax.all_gather(mlp_up, "seq", axis=0, tiled=True),
        preferred_element_type=jnp.float32,
    )
    hidden = jax.nn.gelu(pre_act, approximate=True).astype(jnp.bfloat16)
    columns = hidden
    mlp_out = jnp.dot(
        columns,
        lax.all_gather(mlp_down, "seq", axis=0, tiled=True),
        preferred_element_type=jnp.float32,
    ).astype(jnp.bfloat16)
    return (attended, mlp_out)


def solution(mesh):
    placed = (
        P(("group", "seq"), None),
        P(("group", "seq"), None),
        P(("group", "seq"), None),
        P(),
        P("group"),
        P(),
        P("seq", None),
        P("seq", None),
    )
    return jax.shard_map(
        per_device,
        mesh=mesh,
        in_specs=placed,
        out_specs=(P(("group", "seq"), None), P(("group", "seq"), None)),
        check_vma=False,
    )
```

profile of v0, /device:TPU:0, one launch (start us, length us, event | category | flops | bytes accessed | tf_op | source)
XLA Modules:
  0.0 397.6 jit_solution(10071234965016458596)
XLA Ops:
  13.0 2.0 copy.69
  15.0 2.0 fusion.49
  17.0 70.1 %all-reduce.2 = (bf16[64,768]{1,0:T(8,128)(2,1)}, bf16[64,768]{1,0:T(8,128)(2,1)}, bf16[64,768]{1,0:T(8,128)(2,1)}) all-reduce(f32[64,768]{1,0:T(8,128)} %fusion.47, f32[64,768]{1,0:T(8,128)} %fusion.48, f32[64,768]{1,0:T(8,128)} %fusion.49), channel_id=1, replica_groups=mesh['group'=2,'seq'=16] {'seq'}, use_global_device_ids=true, to_apply=%region_7.8 | all-reduce | flops 147456 | bytes 884736 | tf_op jit(solution)/shard_map/psum | solution.py:108
  91.1 2.4 fusion.37
  97.8 19.8 %collective-permute-done.2 = bf16[2,256,768]{2,1,0:T(8,128)(2,1)} collective-permute-done((bf16[2,256,768]{2,1,0:T(8,128)(2,1)}, bf16[2,256,768]{2,1,0:T(8,128)(2,1)}, u32[]{:S(2)}, u32[]{:S(2)}) %collective-permute-start.2) | collective-permute-done | bytes 786464 | tf_op jit(solution)/shard_map/ppermute | solution.py:31
  117.6 2.1 broadcast_select_fusion
  121.1 17.6 %collective-permute-done.3 = bf16[2,256,768]{2,1,0:T(8,128)(2,1)} collective-permute-done((bf16[2,256,768]{2,1,0:T(8,128)(2,1)}, bf16[2,256,768]{2,1,0:T(8,128)(2,1)}, u32[]{:S(2)}, u32[]{:S(2)}) %collective-permute-start.3) | collective-permute-done | bytes 786464 | tf_op jit(solution)/shard_map/ppermute | solution.py:31
  138.8 2.4 broadcast_select_fusion.1
  142.1 15.3 %collective-permute-start = (bf16[2,128,768]{2,1,0:T(8,128)(2,1)}, bf16[2,128,768]{2,1,0:T(8,128)(2,1)}, u32[]{:S(2)}, u32[]{:S(2)}) collective-permute-start(bf16[2,128,768]{2,1,0:T(8,128)(2,1)} %get-tuple-element.209), channel_id=1, source_target_pairs={{0,1},{1,2},{2,3},{3,4},{4,5},{5,6},{6,7},{7,8},{8,9},{9,10},{10,1... | collective-permute-start | bytes 1179656 | tf_op jit(solution)/shard_map/ppermute | solution.py:19
  157.4 4.5 %collective-permute-start.1 = (bf16[2,128,768]{2,1,0:T(8,128)(2,1)}, bf16[2,128,768]{2,1,0:T(8,128)(2,1)}, u32[]{:S(2)}, u32[]{:S(2)}) collective-permute-start(bf16[2,128,768]{2,1,0:T(8,128)(2,1)} %get-tuple-element.210), channel_id=1, source_target_pairs={{1,0},{2,1},{3,2},{4,3},{5,4},{6,5},{7,6},{8,7},{9,8},{10,9},{11,1... | collective-permute-start | bytes 1179656 | tf_op jit(solution)/shard_map/ppermute | solution.py:21
  176.9 23.6 %all-gather.4 = f32[16,12,64]{2,1,0:T(8,128)S(1)} all-gather(f32[1,12,64]{2,1,0:T(8,128)S(1)} %bitcast.103), channel_id=3, replica_groups=mesh['group'=2,'seq'=16] {'seq'}, dimensions={0}, use_global_device_ids=true | all-gather | bytes 52224 | tf_op jit(solution)/shard_map/all_gather | solution.py:35
  200.6 18.3 %all-gather.3 = f32[16,12,64]{2,1,0:T(8,128)S(1)} all-gather(f32[1,12,64]{2,1,0:T(8,128)S(1)} %bitcast.102), channel_id=2, replica_groups=mesh['group'=2,'seq'=16] {'seq'}, dimensions={0}, use_global_device_ids=true | all-gather | bytes 52224 | tf_op jit(solution)/shard_map/all_gather | solution.py:35
  219.5 2.4 broadcast_select_fusion.2
  222.5 2.4 pad_maximum_fusion.2
  224.9 2.6 copy.71
  227.5 3.5 reshape.91
  231.0 5.1 %fusion.65 = (bf16[2,2,128,12,64]{2,1,4,3,0:T(2,128)(2,1)S(1)}, bf16[2,2,128,12,64]{2,1,4,3,0:T(2,128)(2,1)S(1)}, bf16[2,2,128,12,64]{2,1,4,3,0:T(2,128)(2,1)S(1)}) fusion(bf16[2,4,128,12,64]{2,1,4,3,0:T(4,128)(2,1)} %reshape.91), kind=kLoop, calls=%fused_computation.98 | loop fusion | bytes 4718592 | tf_op jit(solution)/shard_map/slice | solution.py:114
  238.6 2.3 copy.78
  240.9 2.8 reshape.95
  243.7 2.3 copy.77
  246.0 2.7 reshape.94
  248.7 2.3 copy.76
  251.0 2.7 reshape.93
  253.7 39.6 %collective-permute-done.5 = bf16[2,256,768]{2,1,0:T(8,128)(2,1)} collective-permute-done((bf16[2,256,768]{2,1,0:T(8,128)(2,1)}, bf16[2,256,768]{2,1,0:T(8,128)(2,1)}, u32[]{:S(2)}, u32[]{:S(2)}) %collective-permute-start.5) | collective-permute-done | bytes 786464 | tf_op jit(solution)/shard_map/ppermute | solution.py:31
  293.3 2.3 copy.75
  295.6 2.7 reshape.92
  298.3 2.6 fusion.36
  303.6 7.2 %fusion.66 = (f32[2,12,128]{2,1,0:T(8,128)S(1)}, f32[2,12,128,576]{2,3,1,0:T(8,128)}) fusion(bf16[2,64,12,64]{1,3,2,0:T(8,128)(2,1)S(1)} %broadcast_in_dim.97, bf16[2,512,12,64]{1,3,2,0:T(8,128)(2,1)} %get-tuple-element.205, bf16[2,128,12,64]{1,0,3,2:T(2,128)(2,1)S(1)} %copy-done.8), kind=kOutput, calls=%fused_computation.99 | convolution fusion | flops 235340352 | bytes 9252864 | tf_op jit(solution)/shard_map/sub | solution.py:57
  310.9 4.3 %fusion.30 = bf16[2,128,12,64]{1,3,2,0:T(8,128)(2,1)S(1)} fusion(f32[2,12,128,576]{2,3,1,0:T(8,128)} %get-tuple-element.215, f32[2,12,128]{2,1,0:T(8,128)S(1)} %get-tuple-element.214, bf16[2,64,12,64]{1,3,2,0:T(8,128)(2,1)S(1)} %broadcast_in_dim.95, bf16[2,512,12,64]{1,3,2,0:T(8,128)(2,1)} %get-tuple-element.204), kind=kOutput, calls=%fused_computation.42 | convolution fusion | flops 233570304 | bytes 9252864 | tf_op jit(solution)/shard_map/nhqk,nkhd->nqhd/dot_general | solution.py:60
  317.0 32.2 %while.19 = (s32[]{:T(128)}, f32[12,64]{1,0:T(8,128)S(1)}, f32[12,64]{1,0:T(8,128)S(1)}, f32[12,64,64]{2,1,0:T(8,128)S(1)}, f32[16,12,64]{2,1,0:T(8,128)}, /*ind...) while((s32[]{:T(128)}, f32[12,64]{1,0:T(8,128)S(1)}, ...), condition=%wide.region_5.6_spmd, body=%wide.region_4.5_spmd.sunk | while | flops 152069 | bytes 620695 | solution.py:40
  351.2 27.4 %all-gather.9.cloned.1.call-done = bf16[1536,3072]{1,0:T(8,128)(2,1)} async-done(((bf16[96,3072]{1,0:T(8,128)(2,1)}), bf16[1536,3072]{1,0:T(8,128)(2,1)}) %all-gather.9.cloned.1.call-update) | async-done | bytes 9437200 | tf_op jit(solution)/shard_map/all_gather | solution.py:145
  378.6 12.4 %convolution_convert_fusion = bf16[256,1536]{1,0:T(8,128)(2,1)} fusion(bf16[3072,1536]{1,0:T(8,128)(2,1)} %all-gather.11.cloned.1.call-done, bf16[256,1536]{1,0:T(8,128)(2,1)S(1)} %convolution_convert_fusion.1, bf16[1536,3072]{1,0:T(8,128)(2,1)} %all-gather.9.cloned.1.call-done), kind=kOutput, calls=%fused_computation.28 | convolution fusion | flops 4839309312 | bytes 20447232 | tf_op jit(solution)/shard_map/dot_general | solution.py:150
  (128 shorter events, 73.4 us)
Async XLA Ops:
  7.2 343.2 %copy-start = (bf16[768,1536]{1,0:T(8,128)(2,1)S(1)}, bf16[768,1536]{1,0:T(8,128)(2,1)}, u32[]{:S(2)}) copy-start(bf16[768,1536]{1,0:T(8,128)(2,1)} %param.15) | copy-start | bytes 7077892
  7.2 308.7 %all-gather.13.cloned.1.call-start = ((), (), s32[]{:S(2)}) async-start(), calls=%async_computation.2 | async-start | bytes 6684672 | tf_op jit(solution)/shard_map/all_gather | solution.py:35
  9.2 79.7 %copy-start.11 = (s32[64]{0:T(128)}, s32[64]{0:T(128)S(1)}, u32[]{:S(2)}) copy-start(s32[64]{0:T(128)S(1)} %broadcast_subtract_fusion) | copy-start | bytes 772
  15.0 80.0 %copy-start.1 = (bf16[256,768]{1,0:T(8,128)(2,1)S(1)}, bf16[256,768]{1,0:T(8,128)(2,1)}, u32[]{:S(2)}) copy-start(bf16[256,768]{1,0:T(8,128)(2,1)} %param.11) | copy-start | bytes 1179652
  15.0 80.0 %copy-start.2 = (bf16[256,768]{1,0:T(8,128)(2,1)S(1)}, bf16[256,768]{1,0:T(8,128)(2,1)}, u32[]{:S(2)}) copy-start(bf16[256,768]{1,0:T(8,128)(2,1)} %param.12) | copy-start | bytes 1179652
  88.9 7.0 %copy-start.17 = (s32[12]{0:T(128)S(1)}, s32[12]{0:T(128)}, u32[]{:S(2)}) copy-start(s32[12]{0:T(128)} %param.13) | copy-start | bytes 148
  90.2 0.9 copy-start.3
  93.5 257.7 %all-gather.11.cloned.1.call-start = ((), (), s32[]{:S(2)}) async-start(), calls=%async_computation.1 | async-start | bytes 10027008 | tf_op jit(solution)/shard_map/all_gather | solution.py:152
  94.2 284.4 %all-gather.9.cloned.1.call-start = ((), (), s32[]{:S(2)}) async-start(), calls=%async_computation | async-start | bytes 10027008 | tf_op jit(solution)/shard_map/all_gather | solution.py:145
  95.9 21.7 %collective-permute-start.2 = (bf16[2,256,768]{2,1,0:T(8,128)(2,1)}, bf16[2,256,768]{2,1,0:T(8,128)(2,1)}, u32[]{:S(2)}, u32[]{:S(2)}) collective-permute-start(bf16[2,256,768]{2,1,0:T(8,128)(2,1)} %pad_maximum_fusion.9), channel_id=1, source_target_pairs={{0,15},{1,0},{2,1},{3,2},{4,3},{5,4},{6,5},{7,6},{8,7},{9,8},{10,9... | collective-permute-start | bytes 2359304 | tf_op jit(solution)/shard_map/ppermute | solution.py:31
  97.1 0.6 copy-start.15
  119.8 19.0 %collective-permute-start.3 = (bf16[2,256,768]{2,1,0:T(8,128)(2,1)}, bf16[2,256,768]{2,1,0:T(8,128)(2,1)}, u32[]{:S(2)}, u32[]{:S(2)}) collective-permute-start(bf16[2,256,768]{2,1,0:T(8,128)(2,1)} %broadcast_select_fusion), channel_id=1, source_target_pairs={{0,14},{1,15},{2,0},{3,1},{4,2},{5,3},{6,4},{7,5},{8,6},{9,7},{10,... | collective-permute-start | bytes 2359304 | tf_op jit(solution)/shard_map/ppermute | solution.py:31
  121.1 45.5 %copy-start.14 = (pred[12]{0:T(512)(128)(4,1)S(1)}, pred[12]{0:T(512)(128)(4,1)}, u32[]{:S(2)}) copy-start(pred[12]{0:T(512)(128)(4,1)} %get-tuple-element.211) | copy-start | bytes 40
  141.1 78.4 %collective-permute-start.4 = (bf16[2,256,768]{2,1,0:T(8,128)(2,1)}, bf16[2,256,768]{2,1,0:T(8,128)(2,1)}, u32[]{:S(2)}, u32[]{:S(2)}) collective-permute-start(bf16[2,256,768]{2,1,0:T(8,128)(2,1)} %broadcast_select_fusion.1), channel_id=1, source_target_pairs={{0,12},{1,13},{2,14},{3,15},{4,0},{5,1},{6,2},{7,3},{8,4},{9,5},{1... | collective-permute-start | bytes 2359304 | tf_op jit(solution)/shard_map/ppermute | solution.py:31
  142.1 80.4 %collective-permute-start = (bf16[2,128,768]{2,1,0:T(8,128)(2,1)}, bf16[2,128,768]{2,1,0:T(8,128)(2,1)}, u32[]{:S(2)}, u32[]{:S(2)}) collective-permute-start(bf16[2,128,768]{2,1,0:T(8,128)(2,1)} %get-tuple-element.209), channel_id=1, source_target_pairs={{0,1},{1,2},{2,3},{3,4},{4,5},{5,6},{6,7},{7,8},{8,9},{9,10},{10,1... | collective-permute-start | bytes 1179656 | tf_op jit(solution)/shard_map/ppermute | solution.py:19
  157.4 61.5 %copy-start.12 = (s32[64]{0:T(128)S(1)}, s32[64]{0:T(128)}, u32[]{:S(2)}) copy-start(s32[64]{0:T(128)} %copy-done.11) | copy-start | bytes 772
  157.4 65.1 %collective-permute-start.1 = (bf16[2,128,768]{2,1,0:T(8,128)(2,1)}, bf16[2,128,768]{2,1,0:T(8,128)(2,1)}, u32[]{:S(2)}, u32[]{:S(2)}) collective-permute-start(bf16[2,128,768]{2,1,0:T(8,128)(2,1)} %get-tuple-element.210), channel_id=1, source_target_pairs={{1,0},{2,1},{3,2},{4,3},{5,4},{6,5},{7,6},{8,7},{9,8},{10,9},{11,1... | collective-permute-start | bytes 1179656 | tf_op jit(solution)/shard_map/ppermute | solution.py:21
  200.6 18.4 %copy-start.9 = (f32[16,12,64]{2,1,0:T(8,128)}, f32[16,12,64]{2,1,0:T(8,128)S(1)}, u32[]{:S(2)}) copy-start(f32[16,12,64]{2,1,0:T(8,128)S(1)} %all-gather.4) | copy-start | bytes 147460
  218.8 0.7 copy-start.10
  221.9 71.4 %collective-permute-start.5 = (bf16[2,256,768]{2,1,0:T(8,128)(2,1)}, bf16[2,256,768]{2,1,0:T(8,128)(2,1)}, u32[]{:S(2)}, u32[]{:S(2)}) collective-permute-start(bf16[2,256,768]{2,1,0:T(8,128)(2,1)} %broadcast_select_fusion.2), channel_id=1, source_target_pairs={{0,8},{1,9},{2,10},{3,11},{4,12},{5,13},{6,14},{7,15},{8,0},{9,1},... | collective-permute-start | bytes 2359304 | tf_op jit(solution)/shard_map/ppermute | solution.py:31
  298.3 2.6 copy-start.4
  298.3 2.6 copy-start.5
  301.6 1.9 copy-start.7
  301.6 2.0 copy-start.8
  303.6 7.2 %copy-start.6 = (bf16[64,768]{0,1:T(8,128)(2,1)S(1)}, bf16[64,768]{0,1:T(8,128)(2,1)}, u32[]{:S(2)}) copy-start(bf16[64,768]{0,1:T(8,128)(2,1)} %copy.93) | copy-start | bytes 294916
  316.9 32.8 %copy-start.13 = (s32[64]{0:T(128)S(1)}, s32[64]{0:T(128)}, u32[]{:S(2)}) copy-start(s32[64]{0:T(128)} %copy-done.11) | copy-start | bytes 772
  316.9 32.8 %copy-start.16 = (pred[256]{0:T(512)(128)(4,1)S(1)}, pred[256]{0:T(512)(128)(4,1)}, u32[]{:S(2)}) copy-start(pred[256]{0:T(512)(128)(4,1)} %broadcast_compare_fusion) | copy-start | bytes 772
  351.1 39.9 %copy-start.18 = (bf16[256,1536]{1,0:T(8,128)(2,1)}, bf16[256,1536]{1,0:T(8,128)(2,1)S(1)}, u32[]{:S(2)}) copy-start(bf16[256,1536]{1,0:T(8,128)(2,1)S(1)} %convolution_convert_fusion.1) | copy-start | bytes 2359300
Sparse Core Ops, SparseCore 0:
  93.6 83.7 all-gather.12
  179.7 116.0 all-gather.10
  298.1 80.4 all-gather.8
where the time goes:
time: 400 us; the launch traced here: 398 us
  blocking collectives  112 us (28%)
  waiting for transfers between devices  106 us (26%)
  local copies, waits for them, and re-layouts  60.1 us (15%)
  other arithmetic  50.4 us (13%)
  matrix products  34.8 us (9%)
  starting transfers between devices  19.9 us (5%)
  between operations  14.1 us (4%)
    ppermute x4, waiting for transfers between devices, passed_along(): return lax.ppermute(value, axis, pairs)  77.1 us
    psum x1, blocking collectives, per_device(): glob_q, glob_k, glob_v = lax.psum((picked[0], picked[1], picked[2]), 'seq')  70.1 us
    all_gather x2, blocking collectives, merged_2(): gathered = jax.tree.map(lambda a: lax.all_gather(a, axis), part)  41.9 us
    all_gather x1, waiting for transfers between devices, per_device(): lax.all_gather(mlp_up, 'seq', axis=0, tiled=True)  27.4 us
    add x15, other arithmetic, join_partials(): numer_first * scale_first[:, :, None]  20.8 us
    ppermute x1, starting transfers between devices, with_halo(): lax.ppermute(tail, axis, [(i, (i + 1) % count) for i in range(count)])  15.3 us
    dot_general x1, matrix products, per_device(): jnp.dot(columns, lax.all_gather(mlp_down, 'seq', axis=0, tiled=True), pre...  12.4 us
    add x15, other arithmetic, join_partials(): total_first * scale_first + total_second * scale_second  11 us
  transfers between devices with their start and end apart: 9, of which 4 were waited for; matrix products, arithmetic and copies ran while one was open for 29% of the time, Pallas kernels for 0%

commit v1 on v0

--- a/solution.py
+++ b/solution.py
@@ -7,6 +7,27 @@
 DH = 64
 BLK = 128
 GLOBALS = 64
+
+
+def in_order(blocks, dim):
+    blocks = jnp.moveaxis(blocks, 0, dim)
+    dims = blocks.shape
+    return blocks.reshape(*dims[:dim], dims[dim] * dims[dim + 1], *dims[dim + 2 :])
+
+
+def grow_blocks(x, axis):
+    length, mine = (lax.axis_size(axis), lax.axis_index(axis))
+    blocks, bit = (x[None], 1)
+    while bit < length:
+        other = lax.ppermute(blocks, axis, [(i, i ^ bit) for i in range(length)])
+        low = mine & bit == 0
+        blocks = jnp.concatenate([jnp.where(low, blocks, other), jnp.where(low, other, blocks)])
+        bit *= 2
+    return blocks
+
+
+def collect(x, axis, dim):
+    return in_order(grow_blocks(x, axis), dim)
 
 
 def with_halo(cells, sides, width):
@@ -140,11 +161,7 @@
         jnp.bfloat16
     )
     columns = attended
-    pre_act = jnp.dot(
-        columns,
-        lax.all_gather(mlp_up, "seq", axis=0, tiled=True),
-        preferred_element_type=jnp.float32,
-    )
+    pre_act = jnp.dot(columns, collect(mlp_up, "seq", 0), preferred_element_type=jnp.float32)
     hidden = jax.nn.gelu(pre_act, approximate=True).astype(jnp.bfloat16)
     columns = hidden
     mlp_out = jnp.dot(

time: 400 us -> 566 us (1.42)
  waiting for transfers between devices: 106 us -> 263 us
  other arithmetic: 50.4 us -> 68.9 us
  starting transfers between devices: 19.9 us -> 10.2 us
    ppermute x0 -> x4, waiting for transfers between devices: none -> 182 us  [grow_blocks(): other = lax.ppermute(blocks, axis, [(i, i ^ bit) for i in range(length)])]
    all_gather x1 -> x0, waiting for transfers between devices: 27.4 us -> none  [per_device(): lax.all_gather(mlp_up, 'seq', axis=0, tiled=True)]
    ppermute x1, starting transfers between devices: 15.3 us -> 0.51 us  [with_halo(): lax.ppermute(tail, axis, [(i, (i + 1) % count) for i in range(count)])]
    concatenate x0 -> x4, other arithmetic: none -> 9.68 us  [grow_blocks(): jnp.concatenate([jnp.where(low, blocks, other), jnp.where(low, other, blo...]
    select_n x0 -> x4, other arithmetic: none -> 9.27 us  [grow_blocks(): jnp.where(low, blocks, other)]
    unnamed x45 -> x59, local copies, waits for them, and re-layouts: 9.81 us -> 13 us
  transfers between devices with their start and end apart: 9 -> 12, of which waited for: 4 -> 5; matrix products, arithmetic and copies ran while one was open for 29% -> 24% of each run, Pallas kernels for 0% -> 0%
where the time goes in v1:
time: 566 us; the launch traced here: 563 us
  waiting for transfers between devices  263 us (46%)
  blocking collectives  108 us (19%)
  other arithmetic  68.9 us (12%)
  local copies, waits for them, and re-layouts  63.2 us (11%)
  matrix products  35.1 us (6%)
  between operations  14.4 us (3%)
  starting transfers between devices  10.2 us (2%)
    ppermute x4, waiting for transfers between devices, grow_blocks(): other = lax.ppermute(blocks, axis, [(i, i ^ bit) for i in range(length)])  182 us
    ppermute x4, waiting for transfers between devices, passed_along(): return lax.ppermute(value, axis, pairs)  81.1 us
    psum x1, blocking collectives, per_device(): glob_q, glob_k, glob_v = lax.psum((picked[0], picked[1], picked[2]), 'seq')  70.1 us
    all_gather x2, blocking collectives, merged_2(): gathered = jax.tree.map(lambda a: lax.all_gather(a, axis), part)  37.9 us
    add x15, other arithmetic, join_partials(): numer_first * scale_first[:, :, None]  20.7 us
    unnamed x59, local copies, waits for them, and re-layouts  13 us
    dot_general x1, matrix products, per_device(): jnp.dot(columns, lax.all_gather(mlp_down, 'seq', axis=0, tiled=True), pre...  12.4 us
  transfers between devices with their start and end apart: 12, of which 5 were waited for; matrix products, arithmetic and copies ran while one was open for 24% of the time, Pallas kernels for 0%

profile of v1, /device:TPU:0, one launch (start us, length us, event | category | flops | bytes accessed | tf_op | source)
XLA Modules:
  0.0 563.3 jit_solution(5247173403233237808)
XLA Ops:
  11.1 2.0 fusion.48
  16.9 70.1 %all-reduce.2 = (bf16[64,768]{1,0:T(8,128)(2,1)}, bf16[64,768]{1,0:T(8,128)(2,1)}, bf16[64,768]{1,0:T(8,128)(2,1)}) all-reduce(f32[64,768]{1,0:T(8,128)} %fusion.47, f32[64,768]{1,0:T(8,128)} %fusion.48, f32[64,768]{1,0:T(8,128)} %fusion.49), channel_id=1, replica_groups=mesh['group'=2,'seq'=16] {'seq'}, use_global_device_ids=true, to_apply=%region_7.8 | all-reduce | flops 147456 | bytes 884736 | tf_op jit(solution)/shard_map/psum | solution.py:129
  91.0 2.3 fusion.37
  96.0 3.9 collective-permute-start.1
  119.2 18.2 %all-gather.4 = f32[16,12,64]{2,1,0:T(8,128)S(1)} all-gather(f32[1,12,64]{2,1,0:T(8,128)S(1)} %bitcast.109), channel_id=3, replica_groups=mesh['group'=2,'seq'=16] {'seq'}, dimensions={0}, use_global_device_ids=true | all-gather | bytes 52224 | tf_op jit(solution)/shard_map/all_gather | solution.py:56
  137.4 19.6 %all-gather.3 = f32[16,12,64]{2,1,0:T(8,128)S(1)} all-gather(f32[1,12,64]{2,1,0:T(8,128)S(1)} %bitcast.108), channel_id=2, replica_groups=mesh['group'=2,'seq'=16] {'seq'}, dimensions={0}, use_global_device_ids=true | all-gather | bytes 52224 | tf_op jit(solution)/shard_map/all_gather | solution.py:56
  163.7 17.9 %collective-permute-done.3 = bf16[2,256,768]{2,1,0:T(8,128)(2,1)S(1)} collective-permute-done((bf16[2,256,768]{2,1,0:T(8,128)(2,1)S(1)}, bf16[2,256,768]{2,1,0:T(8,128)(2,1)S(1)}, u32[]{:S(2)}, u32[]{:S(2)}) %collective-permute-start.3) | collective-permute-done | bytes 786464 | tf_op jit(solution)/shard_map/ppermute | solution.py:52
  182.4 2.1 broadcast_select_fusion.7
  185.1 2.4 pad_maximum_fusion.5
  187.5 2.6 copy.71
  190.1 3.5 reshape.94
  193.6 5.0 fusion.65
  206.9 7.0 %collective-permute-done.4 = bf16[2,256,768]{2,1,0:T(8,128)(2,1)} collective-permute-done((bf16[2,256,768]{2,1,0:T(8,128)(2,1)}, bf16[2,256,768]{2,1,0:T(8,128)(2,1)}, u32[]{:S(2)}, u32[]{:S(2)}) %collective-permute-start.4) | collective-permute-done | bytes 786464 | tf_op jit(solution)/shard_map/ppermute | solution.py:52
  213.9 2.3 broadcast_select_fusion.8
  217.0 2.5 broadcast_select_fusion.5
  222.2 2.2 collective-permute-start.8
  224.4 2.3 copy.76
  226.7 2.7 reshape.96
  229.4 56.2 %collective-permute-done.5 = bf16[2,256,768]{2,1,0:T(8,128)(2,1)} collective-permute-done((bf16[2,256,768]{2,1,0:T(8,128)(2,1)}, bf16[2,256,768]{2,1,0:T(8,128)(2,1)}, u32[]{:S(2)}, u32[]{:S(2)}) %collective-permute-start.5) | collective-permute-done | bytes 786464 | tf_op jit(solution)/shard_map/ppermute | solution.py:52
  285.6 2.3 copy.75
  287.9 2.8 reshape.95
  290.7 2.7 fusion.36
  297.1 7.7 %fusion.66 = (f32[2,12,128]{2,1,0:T(8,128)}, f32[2,12,128,576]{2,3,1,0:T(8,128)}) fusion(bf16[2,64,12,64]{1,3,2,0:T(8,128)(2,1)} %broadcast_in_dim.100, bf16[2,512,12,64]{1,3,2,0:T(8,128)(2,1)} %get-tuple-element.209, bf16[2,128,12,64]{1,0,3,2:T(2,128)(2,1)} %reshape.99), kind=kOutput, calls=%fused_computation.111 | convolution fusion | flops 235340352 | bytes 9252864 | tf_op jit(solution)/shard_map/sub | solution.py:78
  305.8 4.2 fusion.30
  313.2 12.1 %collective-permute-done.8 = bf16[4,96,3072]{2,1,0:T(8,128)(2,1)} collective-permute-done((bf16[4,96,3072]{2,1,0:T(8,128)(2,1)}, bf16[4,96,3072]{2,1,0:T(8,128)(2,1)}, u32[]{:S(2)}, u32[]{:S(2)}) %collective-permute-start.8) | collective-permute-done | bytes 2359328 | tf_op jit(solution)/shard_map/ppermute | solution.py:22
  325.2 2.3 broadcast_select_fusion.3
  327.5 2.9 pad_maximum_fusion.1
  332.6 32.1 %while.19 = (s32[]{:T(128)}, f32[12,64]{1,0:T(8,128)S(1)}, f32[12,64]{1,0:T(8,128)S(1)}, f32[12,64,64]{2,1,0:T(8,128)S(1)}, f32[16,12,64]{2,1,0:T(8,128)}, /*ind...) while((s32[]{:T(128)}, f32[12,64]{1,0:T(8,128)S(1)}, ...), condition=%wide.region_5.6_spmd, body=%wide.region_4.5_spmd.sunk | while | flops 152069 | bytes 620695 | solution.py:61
  366.8 169.9 %collective-permute-done.9 = bf16[8,96,3072]{2,1,0:T(8,128)(2,1)} collective-permute-done((bf16[8,96,3072]{2,1,0:T(8,128)(2,1)}, bf16[8,96,3072]{2,1,0:T(8,128)(2,1)}, u32[]{:S(2)}, u32[]{:S(2)}) %collective-permute-start.9) | collective-permute-done | bytes 4718624 | tf_op jit(solution)/shard_map/ppermute | solution.py:22
  536.6 3.4 broadcast_select_fusion.1
  540.0 4.0 pad_maximum_fusion
  544.0 12.4 %convolution_convert_fusion = bf16[256,1536]{1,0:T(8,128)(2,1)} fusion(bf16[3072,1536]{1,0:T(8,128)(2,1)} %all-gather.8.cloned.1.call-done, bf16[256,1536]{1,0:T(8,128)(2,1)S(1)} %convolution_convert_fusion.1, bf16[1536,3072]{1,0:T(8,128)(2,1)} %bitcast.99), kind=kOutput, calls=%fused_computation.32 | convolution fusion | flops 4839309312 | bytes 20447232 | tf_op jit(solution)/shard_map/dot_general | solution.py:167
  (155 shorter events, 96.8 us)
Async XLA Ops:
  7.2 358.8 %copy-start = (bf16[768,1536]{1,0:T(8,128)(2,1)S(1)}, bf16[768,1536]{1,0:T(8,128)(2,1)}, u32[]{:S(2)}) copy-start(bf16[768,1536]{1,0:T(8,128)(2,1)} %param.15) | copy-start | bytes 7077892
  7.2 324.4 %all-gather.10.cloned.1.call-start = ((), (), s32[]{:S(2)}) async-start(), calls=%async_computation.1 | async-start | bytes 6684672 | tf_op jit(solution)/shard_map/all_gather | solution.py:56
  9.2 147.8 %copy-start.20 = (s32[64]{0:T(128)}, s32[64]{0:T(128)S(1)}, u32[]{:S(2)}) copy-start(s32[64]{0:T(128)S(1)} %broadcast_subtract_fusion) | copy-start | bytes 772
  11.1 82.4 %copy-start.4 = (bf16[256,768]{1,0:T(8,128)(2,1)S(1)}, bf16[256,768]{1,0:T(8,128)(2,1)}, u32[]{:S(2)}) copy-start(bf16[256,768]{1,0:T(8,128)(2,1)} %param.11) | copy-start | bytes 1179652
  11.1 82.4 %copy-start.5 = (bf16[256,768]{1,0:T(8,128)(2,1)S(1)}, bf16[256,768]{1,0:T(8,128)(2,1)}, u32[]{:S(2)}) copy-start(bf16[256,768]{1,0:T(8,128)(2,1)} %param.12) | copy-start | bytes 1179652
  93.4 450.6 %all-gather.8.cloned.1.call-start = ((), (), s32[]{:S(2)}) async-start(), calls=%async_computation | async-start | bytes 10027008 | tf_op jit(solution)/shard_map/all_gather | solution.py:169
  93.5 65.2 %collective-permute-start.6 = (bf16[1,96,3072]{2,1,0:T(8,128)(2,1)}, bf16[1,96,3072]{2,1,0:T(8,128)(2,1)}, u32[]{:S(2)}, u32[]{:S(2)}) collective-permute-start(bf16[1,96,3072]{2,1,0:T(8,128)(2,1)} %bitcast.107), channel_id=1, source_target_pairs={{0,1},{1,0},{2,3},{3,2},{4,5},{5,4},{6,7},{7,6},{8,9},{9,8},{10,11... | collective-permute-start | bytes 1769480 | tf_op jit(solution)/shard_map/ppermute | solution.py:22
  94.5 62.7 %collective-permute-start.2 = (bf16[2,256,768]{2,1,0:T(8,128)(2,1)}, bf16[2,256,768]{2,1,0:T(8,128)(2,1)}, u32[]{:S(2)}, u32[]{:S(2)}) collective-permute-start(bf16[2,256,768]{2,1,0:T(8,128)(2,1)} %pad_maximum_fusion.13), channel_id=1, source_target_pairs={{0,15},{1,0},{2,1},{3,2},{4,3},{5,4},{6,5},{7,6},{8,7},{9,8},{10,9... | collective-permute-start | bytes 2359304 | tf_op jit(solution)/shard_map/ppermute | solution.py:52
  95.5 89.6 %collective-permute-start = (bf16[2,128,768]{2,1,0:T(8,128)(2,1)}, bf16[2,128,768]{2,1,0:T(8,128)(2,1)}, u32[]{:S(2)}, u32[]{:S(2)}) collective-permute-start(bf16[2,128,768]{2,1,0:T(8,128)(2,1)} %get-tuple-element.217), channel_id=1, source_target_pairs={{0,1},{1,2},{2,3},{3,4},{4,5},{5,6},{6,7},{7,8},{8,9},{9,10},{10,1... | collective-permute-start | bytes 1179656 | tf_op jit(solution)/shard_map/ppermute | solution.py:40
  96.0 89.1 %collective-permute-start.1 = (bf16[2,128,768]{2,1,0:T(8,128)(2,1)}, bf16[2,128,768]{2,1,0:T(8,128)(2,1)}, u32[]{:S(2)}, u32[]{:S(2)}) collective-permute-start(bf16[2,128,768]{2,1,0:T(8,128)(2,1)} %get-tuple-element.218), channel_id=1, source_target_pairs={{1,0},{2,1},{3,2},{4,3},{5,4},{6,5},{7,6},{8,7},{9,8},{10,9},{11,1... | collective-permute-start | bytes 1179656 | tf_op jit(solution)/shard_map/ppermute | solution.py:42
  117.7 41.0 %copy-start.16 = (bf16[96,3072]{1,0:T(8,128)(2,1)S(1)}, bf16[96,3072]{1,0:T(8,128)(2,1)}, u32[]{:S(2)}) copy-start(bf16[96,3072]{1,0:T(8,128)(2,1)} %param.16) | copy-start | bytes 1769476
  137.4 24.3 %copy-start.17 = (f32[16,12,64]{2,1,0:T(8,128)}, f32[16,12,64]{2,1,0:T(8,128)S(1)}, u32[]{:S(2)}) copy-start(f32[16,12,64]{2,1,0:T(8,128)S(1)} %all-gather.4) | copy-start | bytes 147460
  157.0 4.7 copy-start.18
  157.2 25.2 %copy-start.19 = (pred[768]{0:T(1024)(128)(4,1)S(1)}, pred[768]{0:T(1024)(128)(4,1)}, u32[]{:S(2)}) copy-start(pred[768]{0:T(1024)(128)(4,1)} %broadcast_in_dim.92) | copy-start | bytes 2308
  157.2 25.2 %copy-start.23 = (pred[768]{0:T(1024)(128)(4,1)S(1)}, pred[768]{0:T(1024)(128)(4,1)}, u32[]{:S(2)}) copy-start(pred[768]{0:T(1024)(128)(4,1)} %broadcast_in_dim.89) | copy-start | bytes 2308
  158.4 23.1 %collective-permute-start.3 = (bf16[2,256,768]{2,1,0:T(8,128)(2,1)S(1)}, bf16[2,256,768]{2,1,0:T(8,128)(2,1)S(1)}, u32[]{:S(2)}, u32[]{:S(2)}) collective-permute-start(bf16[2,256,768]{2,1,0:T(8,128)(2,1)S(1)} %broadcast_select_fusion.6), channel_id=1, source_target_pairs={{0,14},{1,15},{2,0},{3,1},{4,2},{5,3},{6,4},{7,5},{8,6},{9,7},{10,... | collective-permute-start | bytes 2359304 | tf_op jit(solution)/shard_map/ppermute | solution.py:52
  161.7 55.3 %collective-permute-start.7 = (bf16[2,96,3072]{2,1,0:T(8,128)(2,1)}, bf16[2,96,3072]{2,1,0:T(8,128)(2,1)}, u32[]{:S(2)}, u32[]{:S(2)}) collective-permute-start(bf16[2,96,3072]{2,1,0:T(8,128)(2,1)} %pad_maximum_fusion.12), channel_id=1, source_target_pairs={{0,2},{1,3},{2,0},{3,1},{4,6},{5,7},{6,4},{7,5},{8,10},{9,11},{10,... | collective-permute-start | bytes 3538952 | tf_op jit(solution)/shard_map/ppermute | solution.py:22
  184.5 29.4 %collective-permute-start.4 = (bf16[2,256,768]{2,1,0:T(8,128)(2,1)}, bf16[2,256,768]{2,1,0:T(8,128)(2,1)}, u32[]{:S(2)}, u32[]{:S(2)}) collective-permute-start(bf16[2,256,768]{2,1,0:T(8,128)(2,1)} %broadcast_select_fusion.7), channel_id=1, source_target_pairs={{0,12},{1,13},{2,14},{3,15},{4,0},{5,1},{6,2},{7,3},{8,4},{9,5},{1... | collective-permute-start | bytes 2359304 | tf_op jit(solution)/shard_map/ppermute | solution.py:52
  201.9 12.0 %copy-start.22 = (pred[768]{0:T(1024)(128)(4,1)S(1)}, pred[768]{0:T(1024)(128)(4,1)}, u32[]{:S(2)}) copy-start(pred[768]{0:T(1024)(128)(4,1)} %broadcast_in_dim.86) | copy-start | bytes 2308
  216.2 69.4 %collective-permute-start.5 = (bf16[2,256,768]{2,1,0:T(8,128)(2,1)}, bf16[2,256,768]{2,1,0:T(8,128)(2,1)}, u32[]{:S(2)}, u32[]{:S(2)}) collective-permute-start(bf16[2,256,768]{2,1,0:T(8,128)(2,1)} %broadcast_select_fusion.8), channel_id=1, source_target_pairs={{0,8},{1,9},{2,10},{3,11},{4,12},{5,13},{6,14},{7,15},{8,0},{9,1},... | collective-permute-start | bytes 2359304 | tf_op jit(solution)/shard_map/ppermute | solution.py:52
  222.2 103.0 %collective-permute-start.8 = (bf16[4,96,3072]{2,1,0:T(8,128)(2,1)}, bf16[4,96,3072]{2,1,0:T(8,128)(2,1)}, u32[]{:S(2)}, u32[]{:S(2)}) collective-permute-start(bf16[4,96,3072]{2,1,0:T(8,128)(2,1)} %pad_maximum_fusion.3), channel_id=1, source_target_pairs={{0,4},{1,5},{2,6},{3,7},{4,0},{5,1},{6,2},{7,3},{8,12},{9,13},{10,... | collective-permute-start | bytes 7077896 | tf_op jit(solution)/shard_map/ppermute | solution.py:22
  290.7 2.7 copy-start.10
  290.7 2.8 copy-start.11
  290.7 2.9 copy-start.12
  327.5 2.9 copy-start.1
  327.5 3.6 copy-start.3
  331.1 205.5 %collective-permute-start.9 = (bf16[8,96,3072]{2,1,0:T(8,128)(2,1)}, bf16[8,96,3072]{2,1,0:T(8,128)(2,1)}, u32[]{:S(2)}, u32[]{:S(2)}) collective-permute-start(bf16[8,96,3072]{2,1,0:T(8,128)(2,1)} %pad_maximum_fusion.1), channel_id=1, source_target_pairs={{0,8},{1,9},{2,10},{3,11},{4,12},{5,13},{6,14},{7,15},{8,0},{9,1},... | collective-permute-start | bytes 14155784 | tf_op jit(solution)/shard_map/ppermute | solution.py:22
  332.6 32.7 %copy-start.14 = (bf16[256,768]{1,0:T(8,128)(2,1)S(1)}, bf16[256,768]{1,0:T(8,128)(2,1)}, u32[]{:S(2)}) copy-start(bf16[256,768]{1,0:T(8,128)(2,1)} %copy.92) | copy-start | bytes 1179652
  332.6 32.7 %copy-start.21 = (s32[64]{0:T(128)S(1)}, s32[64]{0:T(128)}, u32[]{:S(2)}) copy-start(s32[64]{0:T(128)} %copy-done.20) | copy-start | bytes 772
  332.6 32.7 %copy-start.24 = (pred[256]{0:T(512)(128)(4,1)S(1)}, pred[256]{0:T(512)(128)(4,1)}, u32[]{:S(2)}) copy-start(pred[256]{0:T(512)(128)(4,1)} %broadcast_compare_fusion) | copy-start | bytes 772
  365.3 171.3 %copy-start.2 = (bf16[4,96,3072]{2,1,0:T(8,128)(2,1)S(1)}, bf16[4,96,3072]{2,1,0:T(8,128)(2,1)}, u32[]{:S(2)}) copy-start(bf16[4,96,3072]{2,1,0:T(8,128)(2,1)} %copy-done.1) | copy-start | bytes 7077892
  366.7 177.3 %copy-start.25 = (bf16[256,1536]{1,0:T(8,128)(2,1)}, bf16[256,1536]{1,0:T(8,128)(2,1)S(1)}, u32[]{:S(2)}) copy-start(bf16[256,1536]{1,0:T(8,128)(2,1)S(1)} %convolution_convert_fusion.1) | copy-start | bytes 2359300
  (6 other events, 7.5 us)
Sparse Core Ops, SparseCore 0:
  93.5 67.3 all-gather.9
  163.2 130.5 all-gather.7
